TPU v7x, 32 devices: a whole 2x2x4 slice. The times are simulated.
32 devices in a mesh: dp: 16 (over z, y, x), tensor: 2 (over core).
Axes of the slice: x: 2, y: 2, z: 4, core: 2. Of those that a mesh axis runs over, the one named last changes fastest.
Arguments:
- tokens: bfloat16 [4, 16, 2048, 1024], P(None, 'dp', None, 'tensor'), may hold values from -40 to 40
- routed: int32 [4, 16, 256], P(None, 'dp'), may hold values from 0 to 2047, as said below
- w_query: bfloat16 [1024, 1024], P('dp', 'tensor'), may hold values from -0.1875 to 0.1875
- w_key: bfloat16 [1024, 1024], P('dp', 'tensor'), may hold values from -0.1875 to 0.1875
- w_value: bfloat16 [1024, 1024], P('dp', 'tensor'), may hold values from -0.1875 to 0.1875
- w_out: bfloat16 [1024, 1024], P('tensor', 'dp'), may hold values from -1 to 1
- w_up: bfloat16 [1024, 4096], P('dp', 'tensor'), may hold values from -0.1875 to 0.1875
- w_down: bfloat16 [4096, 1024], P('tensor', 'dp'), may hold values from -0.09375 to 0.09375
- w_route: bfloat16 [1024], P('dp'), may hold values from -0.09375 to 0.09375
- gain_attn: bfloat16 [1024], P('dp'), may hold values from 0.099609375 to 1.8984375
- gain_mlp: bfloat16 [1024], P('dp'), may hold values from 0.099609375 to 1.8984375
- cotangent: bfloat16 [4, 16, 2048, 1024], P(None, 'dp', None, 'tensor'), may hold values from -6 to 6
Outputs:
- output: bfloat16 [4, 16, 2048, 1024], P(None, 'dp', None, 'tensor')
- input_grad: bfloat16 [4, 16, 2048, 1024], P(None, 'dp', None, 'tensor')
- grad_query: float32 [1024, 1024], P('dp', 'tensor')
- grad_key: float32 [1024, 1024], P('dp', 'tensor')
- grad_value: float32 [1024, 1024], P('dp', 'tensor')
- grad_out: float32 [1024, 1024], P('tensor', 'dp')
- grad_up: float32 [1024, 4096], P('dp', 'tensor')
- grad_down: float32 [4096, 1024], P('tensor', 'dp')
- grad_route: float32 [1024], P('dp')
- grad_gain_attn: float32 [1024], P('dp')
- grad_gain_mlp: float32 [1024], P('dp')
Inputs may be any that keep to these rules, and one draw needn't show every extreme that they name: Each row of routed holds 256 different positions of its sequence in rising order.
All inputs are finite; a program needn't handle non-finite values.
Results may differ from a plain program's by a relative error of at most 0.02.
Values may be sent and summed in bfloat16 or wider, within the bound.
A program may use at most 192 MiB of HBM per device.

v0:
```python
import jax
import jax.numpy as jnp
from jax import lax
from jax.sharding import PartitionSpec as P

HD = 64
eps_norm = 1e-05


def rms_norm(values, gain):
    return values * lax.rsqrt(jnp.mean(values * values, -1, keepdims=True) + eps_norm) * gain


def dense(left, right):
    return jnp.dot(left, right, preferred_element_type=jnp.float32)


def shards(
    tokens,
    routed,
    w_query,
    w_key,
    w_value,
    w_out,
    w_up,
    w_down,
    w_route,
    gain_attn,
    gain_mlp,
    cotangent,
):
    half_width = tokens.shape[3]
    capacity = routed.shape[2]
    offset = lax.axis_index("tensor") * half_width
    width = half_width * lax.axis_size("tensor")
    score_scale = HD ** (-0.5)
    causal = lax.broadcasted_iota(jnp.int32, (capacity, capacity), 0) >= lax.broadcasted_iota(
        jnp.int32, (capacity, capacity), 1
    )

    def sequence_step(gradients, weight_rows, weight_cols, tok_seq, chosen, cot_seq):
        full_query, full_key, full_value, full_up, full_route, full_gain1, full_gain2 = weight_rows
        full_out, full_down = weight_cols
        g_query, g_key, g_value, g_up, g_route, g_gain1, g_gain2, g_out, g_down = gradients
        route_f32 = full_route.astype(jnp.float32)
        gain1_f32 = full_gain1.astype(jnp.float32)
        gain2_f32 = full_gain2.astype(jnp.float32)
        rows_half = jnp.take(tok_seq, chosen, axis=0)
        cot_half = jnp.take(cot_seq, chosen, axis=0)
        routed_rows, cot_rows = (
            lax.all_gather(rows_half, "tensor", axis=1, tiled=True),
            lax.all_gather(cot_half, "tensor", axis=1, tiled=True),
        )
        rows_f32 = routed_rows.astype(jnp.float32)
        rows_half_f32 = rows_half.astype(jnp.float32)
        cot_half_f32 = cot_half.astype(jnp.float32)
        route_logit = dense(routed_rows, full_route)
        route_gate = jax.nn.sigmoid(route_logit)
        normed = rms_norm(rows_f32, gain1_f32).astype(jnp.bfloat16)
        queries = dense(normed, full_query).astype(jnp.bfloat16).reshape(capacity, -1, HD)
        key_rows = dense(normed, full_key).astype(jnp.bfloat16).reshape(capacity, -1, HD)
        value_rows = dense(normed, full_value).astype(jnp.bfloat16).reshape(capacity, -1, HD)
        scores = (
            jnp.einsum("qhd,khd->hqk", queries, key_rows, preferred_element_type=jnp.float32)
            * score_scale
        )
        scores = jnp.where(causal[None], scores, -1e30)
        log_total = jax.nn.logsumexp(scores, axis=-1, keepdims=True)
        probs_low = jnp.exp(scores - log_total).astype(jnp.bfloat16)
        mixed_heads = jnp.einsum(
            "hqk,khd->qhd", probs_low, value_rows, preferred_element_type=jnp.float32
        )
        mixed_heads = mixed_heads.astype(jnp.bfloat16).reshape(capacity, -1)
        attended = lax.psum(dense(mixed_heads, full_out).astype(jnp.bfloat16), "tensor").astype(
            jnp.float32
        )
        hidden = rows_f32 + attended
        normed2 = rms_norm(hidden, gain2_f32).astype(jnp.bfloat16)
        up_proj = dense(normed2, full_up)
        activated = jax.nn.gelu(up_proj).astype(jnp.bfloat16)
        down_out = lax.psum(dense(activated, full_down).astype(jnp.bfloat16), "tensor").astype(
            jnp.float32
        )
        branch = attended + down_out
        branch_half = lax.dynamic_slice_in_dim(branch, offset, half_width, 1)
        d_logit = (
            jnp.sum(cot_rows.astype(jnp.float32) * branch, -1) * route_gate * (1.0 - route_gate)
        )
        new_rows = (rows_half_f32 + route_gate[:, None] * branch_half).astype(jnp.bfloat16)
        out_seq = tok_seq.at[chosen].set(new_rows)
        cot_f32 = cot_rows.astype(jnp.float32)
        d_branch = route_gate[:, None] * cot_f32
        d_down = d_branch.astype(jnp.bfloat16)
        up_again = dense(lax.optimization_barrier(normed2), full_up)
        act_again = jax.nn.gelu(up_again).astype(jnp.bfloat16)
        g_down = g_down + dense(act_again.T, d_down)
        d_act = dense(d_down, full_down.T)
        gelu_value, gelu_back = jax.vjp(jax.nn.gelu, up_again)
        d_upper = gelu_back(d_act)[0].astype(jnp.bfloat16)
        g_up = g_up + dense(normed2.T, d_upper)
        d_normed2 = lax.psum(dense(d_upper, full_up.T).astype(jnp.bfloat16), "tensor").astype(
            jnp.float32
        )
        norm2_value, norm2_back = jax.vjp(rms_norm, hidden, gain2_f32)
        d_hidden, d_gain2 = norm2_back(d_normed2)
        g_gain2 = g_gain2 + d_gain2
        d_attended = (d_branch + d_hidden).astype(jnp.bfloat16)
        g_out = g_out + dense(mixed_heads.T, d_attended)
        d_mixed = dense(d_attended, full_out.T).astype(jnp.bfloat16).reshape(capacity, -1, HD)
        scores_again = (
            jnp.einsum("qhd,khd->hqk", queries, key_rows, preferred_element_type=jnp.float32)
            * score_scale
        )
        scores_again = jnp.where(causal[None], scores_again, -1e30)
        attn_probs = jnp.exp(scores_again - log_total)
        probs_again = attn_probs.astype(jnp.bfloat16)
        d_values = jnp.einsum(
            "hqk,qhd->khd", probs_again, d_mixed, preferred_element_type=jnp.float32
        )
        d_values = d_values.astype(jnp.bfloat16).reshape(capacity, -1)
        d_probs = jnp.einsum(
            "qhd,khd->hqk", d_mixed, value_rows, preferred_element_type=jnp.float32
        )
        d_scores = attn_probs * (d_probs - jnp.sum(d_probs * attn_probs, -1, keepdims=True))
        d_scores = d_scores.astype(jnp.bfloat16)
        d_queries = (
            jnp.einsum("hqk,khd->qhd", d_scores, key_rows, preferred_element_type=jnp.float32)
            * score_scale
        )
        d_queries = d_queries.astype(jnp.bfloat16).reshape(capacity, -1)
        d_keys = (
            jnp.einsum("hqk,qhd->khd", d_scores, queries, preferred_element_type=jnp.float32)
            * score_scale
        )
        d_keys = d_keys.astype(jnp.bfloat16).reshape(capacity, -1)
        g_query = g_query + dense(normed.T, d_queries)
        g_key = g_key + dense(normed.T, d_keys)
        g_value = g_value + dense(normed.T, d_values)
        partial_normed = (
            dense(d_queries, full_query.T)
            + dense(d_keys, full_key.T)
            + dense(d_values, full_value.T)
        )
        d_hidden_half = lax.dynamic_slice_in_dim(d_hidden, offset, half_width, 1)
        route_half = lax.dynamic_slice_in_dim(route_f32, offset, half_width, 0)
        d_normed = lax.psum(partial_normed.astype(jnp.bfloat16), "tensor").astype(jnp.float32)
        norm1_value, norm1_back = jax.vjp(rms_norm, rows_f32, gain1_f32)
        d_rows_norm, d_gain1 = norm1_back(d_normed)
        g_gain1 = g_gain1 + d_gain1
        d_norm_half = lax.dynamic_slice_in_dim(d_rows_norm, offset, half_width, 1)
        g_route = g_route + jnp.dot(
            rows_f32.T, d_logit, precision=lax.Precision.HIGHEST, preferred_element_type=jnp.float32
        )
        d_half = d_hidden_half + d_norm_half + d_logit[:, None] * route_half[None, :]
        grad_rows_new = (cot_half_f32 + d_half).astype(jnp.bfloat16)
        grad_seq = cot_seq.at[chosen].set(grad_rows_new)
        new_gradients = (g_query, g_key, g_value, g_up, g_route, g_gain1, g_gain2, g_out, g_down)
        return (new_gradients, out_seq, grad_seq)

    def micro_step(gradients, micro_inputs):
        tok_micro, routed_micro, cot_micro = micro_inputs
        weight_rows = (
            lax.all_gather(w_query, "dp", axis=0, tiled=True),
            lax.all_gather(w_key, "dp", axis=0, tiled=True),
            lax.all_gather(w_value, "dp", axis=0, tiled=True),
            lax.all_gather(w_up, "dp", axis=0, tiled=True),
            lax.all_gather(w_route, "dp", axis=0, tiled=True),
            lax.all_gather(gain_attn, "dp", axis=0, tiled=True),
            lax.all_gather(gain_mlp, "dp", axis=0, tiled=True),
        )
        weight_cols = (
            lax.all_gather(w_out, "dp", axis=1, tiled=True),
            lax.all_gather(w_down, "dp", axis=1, tiled=True),
        )

        def sequence_scan(carried, seq_inputs):
            tok_seq, chosen, cot_seq = seq_inputs
            updated, out_seq, grad_seq = sequence_step(
                carried, weight_rows, weight_cols, tok_seq, chosen, cot_seq
            )
            return (updated, (out_seq, grad_seq))

        gradients, seq_results = lax.scan(
            sequence_scan, gradients, (tok_micro, routed_micro, cot_micro)
        )
        return (gradients, seq_results)

    zero_grads = (
        jnp.zeros((width, w_query.shape[1]), jnp.float32),
        jnp.zeros((width, w_key.shape[1]), jnp.float32),
        jnp.zeros((width, w_value.shape[1]), jnp.float32),
        jnp.zeros((width, w_up.shape[1]), jnp.float32),
        jnp.zeros((width,), jnp.float32),
        jnp.zeros((width,), jnp.float32),
        jnp.zeros((width,), jnp.float32),
        jnp.zeros((w_out.shape[0], width), jnp.float32),
        jnp.zeros((w_down.shape[0], width), jnp.float32),
    )
    totals, results = lax.scan(micro_step, zero_grads, (tokens, routed, cotangent))
    output, input_grad = results
    g_query, g_key, g_value, g_up, g_route, g_gain1, g_gain2, g_out, g_down = totals
    grad_query, grad_key, grad_value, grad_up, grad_route, grad_gain_attn, grad_gain_mlp = (
        lax.psum_scatter(g_query, "dp", scatter_dimension=0, tiled=True),
        lax.psum_scatter(g_key, "dp", scatter_dimension=0, tiled=True),
        lax.psum_scatter(g_value, "dp", scatter_dimension=0, tiled=True),
        lax.psum_scatter(g_up, "dp", scatter_dimension=0, tiled=True),
        lax.psum_scatter(g_route, "dp", scatter_dimension=0, tiled=True),
        lax.psum_scatter(g_gain1, "dp", scatter_dimension=0, tiled=True),
        lax.psum_scatter(g_gain2, "dp", scatter_dimension=0, tiled=True),
    )
    grad_out, grad_down = (
        lax.psum_scatter(g_out, "dp", scatter_dimension=1, tiled=True),
        lax.psum_scatter(g_down, "dp", scatter_dimension=1, tiled=True),
    )
    return (
        output,
        input_grad,
        grad_query,
        grad_key,
        grad_value,
        grad_out,
        grad_up,
        grad_down,
        grad_route,
        grad_gain_attn,
        grad_gain_mlp,
    )


def solution(mesh):
    placed = (
        P(None, "dp", None, "tensor"),
        P(None, "dp", None),
        P("dp", "tensor"),
        P("dp", "tensor"),
        P("dp", "tensor"),
        P("tensor", "dp"),
        P("dp", "tensor"),
        P("tensor", "dp"),
        P("dp"),
        P("dp"),
        P("dp"),
        P(None, "dp", None, "tensor"),
    )
    return jax.shard_map(
        shards,
        mesh=mesh,
        in_specs=placed,
        out_specs=(
            P(None, "dp", None, "tensor"),
            P(None, "dp", None, "tensor"),
            P("dp", "tensor"),
            P("dp", "tensor"),
            P("dp", "tensor"),
            P("tensor", "dp"),
            P("dp", "tensor"),
            P("tensor", "dp"),
            P("dp"),
            P("dp"),
            P("dp"),
        ),
        check_vma=False,
    )
```

profile of v0, /device:TPU:10, one launch (start us, length us, event | category | flops | bytes accessed | tf_op | source)
XLA Modules:
  0.0 2646.1 jit_solution(17404735948335513344)
XLA Ops:
  8.1 1940.2 %while.33 = (s32[]{:T(128)}, f32[1024,512]{1,0:T(8,128)}, f32[1024,512]{1,0:T(8,128)}, f32[1024,512]{1,0:T(8,128)}, f32[1024,2048]{1,0:T(8,128)}, /*index=5*/f32...) while((s32[]{:T(128)}, f32[1024,512]{1,0:T(8,128)}, ...), condition=%wide.region_17.19_spmd.clone, body=%wide.region_0.18_spmd.clone.sunk | while | flops 11211988992 | bytes 388675808 | solution.py:199
  25.8 31.6 %all-reduce.14 = (bf16[1024]{0:T(1024)(128)(2,1)S(1)}, bf16[1024]{0:T(1024)(128)(2,1)S(1)}, bf16[1024]{0:T(1024)(128)(2,1)S(1)}) all-reduce(bf16[1024]{0:T(1024)(128)(2,1)S(1)} %dynamic-update-slice.9, bf16[1024]{0:T(1024)(128)(2,1)S(1)} %dynamic-update-slice.10, ...), channel_id=1, replica_groups=mesh['dp'=16,'tensor'=2] {'dp'}, use_global_device_ids=true, to_apply=%add.1 | all-reduce | flops 3072 | bytes 12288 | tf_op jit(solution)/shard_map/while
  57.4 10.1 all-gather.9.cloned.1.call-done
  69.3 55.2 %all-gather.7.cloned.1.call-done = bf16[1024,512]{1,0:T(8,128)(2,1)} async-done(((bf16[64,512]{1,0:T(8,128)(2,1)}), bf16[1024,512]{1,0:T(8,128)(2,1)}) %all-gather.7.cloned.1.call-update) | async-done | bytes 1048592 | tf_op jit(solution)/shard_map/while/body/eval_jaxpr/all_gather | solution.py:164
  126.3 55.0 %all-gather.11.cloned.1.call-done = bf16[1024,512]{1,0:T(8,128)(2,1)} async-done(((bf16[64,512]{1,0:T(8,128)(2,1)}), bf16[1024,512]{1,0:T(8,128)(2,1)}) %all-gather.11.cloned.1.call-update) | async-done | bytes 1048592 | tf_op jit(solution)/shard_map/while/body/eval_jaxpr/all_gather | solution.py:165
  184.5 53.5 %all-gather.13.cloned.1.call-done = bf16[512,1024]{0,1:T(8,128)(2,1)} async-done(((bf16[512,64]{0,1:T(8,128)(2,1)}), bf16[512,1024]{0,1:T(8,128)(2,1)}) %all-gather.13.cloned.1.call-update) | async-done | bytes 1048592 | tf_op jit(solution)/shard_map/while/body/eval_jaxpr/all_gather | solution.py:172
  245.8 13.8 all-reduce.20.cloned.1.call-done
  263.0 76.7 %all-gather.15.cloned.1.call-done = bf16[1024,2048]{1,0:T(8,128)(2,1)} async-done(((bf16[64,2048]{1,0:T(8,128)(2,1)}), bf16[1024,2048]{1,0:T(8,128)(2,1)}) %all-gather.15.cloned.1.call-update) | async-done | bytes 4194320 | tf_op jit(solution)/shard_map/while/body/eval_jaxpr/all_gather | solution.py:166
  339.6 4.9 fusion.230
  344.5 73.0 %all-gather.17.cloned.1.call-done = bf16[2048,1024]{0,1:T(8,128)(2,1)} async-done(((bf16[2048,64]{0,1:T(8,128)(2,1)}), bf16[2048,1024]{0,1:T(8,128)(2,1)}) %all-gather.17.cloned.1.call-update) | async-done | bytes 4194320 | tf_op jit(solution)/shard_map/while/body/eval_jaxpr/all_gather | solution.py:173
  417.5 7.0 convolution_convert_fusion.24
  424.5 5.3 fusion.231
  433.0 6.1 select_add_fusion.21
  439.1 5.3 select_add_fusion.26
  444.4 7.3 all-reduce.22.cloned.1.call-done
  478.5 7.4 all-reduce.24.cloned.1.call-done
  510.9 31.5 %all-reduce.14 = (bf16[1024]{0:T(1024)(128)(2,1)S(1)}, bf16[1024]{0:T(1024)(128)(2,1)S(1)}, bf16[1024]{0:T(1024)(128)(2,1)S(1)}) all-reduce(bf16[1024]{0:T(1024)(128)(2,1)S(1)} %dynamic-update-slice.9, bf16[1024]{0:T(1024)(128)(2,1)S(1)} %dynamic-update-slice.10, ...), channel_id=1, replica_groups=mesh['dp'=16,'tensor'=2] {'dp'}, use_global_device_ids=true, to_apply=%add.1 | all-reduce | flops 3072 | bytes 12288 | tf_op jit(solution)/shard_map/while
  542.4 9.7 all-gather.9.cloned.1.call-done
  554.0 55.2 %all-gather.7.cloned.1.call-done = bf16[1024,512]{1,0:T(8,128)(2,1)} async-done(((bf16[64,512]{1,0:T(8,128)(2,1)}), bf16[1024,512]{1,0:T(8,128)(2,1)}) %all-gather.7.cloned.1.call-update) | async-done | bytes 1048592 | tf_op jit(solution)/shard_map/while/body/eval_jaxpr/all_gather | solution.py:164
  611.0 54.9 %all-gather.11.cloned.1.call-done = bf16[1024,512]{1,0:T(8,128)(2,1)} async-done(((bf16[64,512]{1,0:T(8,128)(2,1)}), bf16[1024,512]{1,0:T(8,128)(2,1)}) %all-gather.11.cloned.1.call-update) | async-done | bytes 1048592 | tf_op jit(solution)/shard_map/while/body/eval_jaxpr/all_gather | solution.py:165
  669.1 53.7 %all-gather.13.cloned.1.call-done = bf16[512,1024]{0,1:T(8,128)(2,1)} async-done(((bf16[512,64]{0,1:T(8,128)(2,1)}), bf16[512,1024]{0,1:T(8,128)(2,1)}) %all-gather.13.cloned.1.call-update) | async-done | bytes 1048592 | tf_op jit(solution)/shard_map/while/body/eval_jaxpr/all_gather | solution.py:172
  730.3 14.0 all-reduce.20.cloned.1.call-done
  747.7 76.7 %all-gather.15.cloned.1.call-done = bf16[1024,2048]{1,0:T(8,128)(2,1)} async-done(((bf16[64,2048]{1,0:T(8,128)(2,1)}), bf16[1024,2048]{1,0:T(8,128)(2,1)}) %all-gather.15.cloned.1.call-update) | async-done | bytes 4194320 | tf_op jit(solution)/shard_map/while/body/eval_jaxpr/all_gather | solution.py:166
  824.3 4.9 fusion.230
  829.2 72.8 %all-gather.17.cloned.1.call-done = bf16[2048,1024]{0,1:T(8,128)(2,1)} async-done(((bf16[2048,64]{0,1:T(8,128)(2,1)}), bf16[2048,1024]{0,1:T(8,128)(2,1)}) %all-gather.17.cloned.1.call-update) | async-done | bytes 4194320 | tf_op jit(solution)/shard_map/while/body/eval_jaxpr/all_gather | solution.py:173
  902.1 7.0 convolution_convert_fusion.24
  909.1 5.3 fusion.231
  917.6 8.6 select_add_fusion.21
  926.2 8.6 select_add_fusion.26
  963.0 7.4 all-reduce.24.cloned.1.call-done
  995.6 31.4 %all-reduce.14 = (bf16[1024]{0:T(1024)(128)(2,1)S(1)}, bf16[1024]{0:T(1024)(128)(2,1)S(1)}, bf16[1024]{0:T(1024)(128)(2,1)S(1)}) all-reduce(bf16[1024]{0:T(1024)(128)(2,1)S(1)} %dynamic-update-slice.9, bf16[1024]{0:T(1024)(128)(2,1)S(1)} %dynamic-update-slice.10, ...), channel_id=1, replica_groups=mesh['dp'=16,'tensor'=2] {'dp'}, use_global_device_ids=true, to_apply=%add.1 | all-reduce | flops 3072 | bytes 12288 | tf_op jit(solution)/shard_map/while
  1027.0 10.0 all-gather.9.cloned.1.call-done
  1038.9 55.0 %all-gather.7.cloned.1.call-done = bf16[1024,512]{1,0:T(8,128)(2,1)} async-done(((bf16[64,512]{1,0:T(8,128)(2,1)}), bf16[1024,512]{1,0:T(8,128)(2,1)}) %all-gather.7.cloned.1.call-update) | async-done | bytes 1048592 | tf_op jit(solution)/shard_map/while/body/eval_jaxpr/all_gather | solution.py:164
  1095.7 55.0 %all-gather.11.cloned.1.call-done = bf16[1024,512]{1,0:T(8,128)(2,1)} async-done(((bf16[64,512]{1,0:T(8,128)(2,1)}), bf16[1024,512]{1,0:T(8,128)(2,1)}) %all-gather.11.cloned.1.call-update) | async-done | bytes 1048592 | tf_op jit(solution)/shard_map/while/body/eval_jaxpr/all_gather | solution.py:165
  1153.9 53.7 %all-gather.13.cloned.1.call-done = bf16[512,1024]{0,1:T(8,128)(2,1)} async-done(((bf16[512,64]{0,1:T(8,128)(2,1)}), bf16[512,1024]{0,1:T(8,128)(2,1)}) %all-gather.13.cloned.1.call-update) | async-done | bytes 1048592 | tf_op jit(solution)/shard_map/while/body/eval_jaxpr/all_gather | solution.py:172
  1215.3 14.0 all-reduce.20.cloned.1.call-done
  1232.7 76.7 %all-gather.15.cloned.1.call-done = bf16[1024,2048]{1,0:T(8,128)(2,1)} async-done(((bf16[64,2048]{1,0:T(8,128)(2,1)}), bf16[1024,2048]{1,0:T(8,128)(2,1)}) %all-gather.15.cloned.1.call-update) | async-done | bytes 4194320 | tf_op jit(solution)/shard_map/while/body/eval_jaxpr/all_gather | solution.py:166
  1309.3 4.9 fusion.230
  1314.2 73.0 %all-gather.17.cloned.1.call-done = bf16[2048,1024]{0,1:T(8,128)(2,1)} async-done(((bf16[2048,64]{0,1:T(8,128)(2,1)}), bf16[2048,1024]{0,1:T(8,128)(2,1)}) %all-gather.17.cloned.1.call-update) | async-done | bytes 4194320 | tf_op jit(solution)/shard_map/while/body/eval_jaxpr/all_gather | solution.py:173
  1387.2 7.0 convolution_convert_fusion.24
  1394.2 5.3 fusion.231
  1402.7 8.6 select_add_fusion.21
  1411.3 8.7 select_add_fusion.26
  1448.2 7.4 all-reduce.24.cloned.1.call-done
  1480.7 31.4 %all-reduce.14 = (bf16[1024]{0:T(1024)(128)(2,1)S(1)}, bf16[1024]{0:T(1024)(128)(2,1)S(1)}, bf16[1024]{0:T(1024)(128)(2,1)S(1)}) all-reduce(bf16[1024]{0:T(1024)(128)(2,1)S(1)} %dynamic-update-slice.9, bf16[1024]{0:T(1024)(128)(2,1)S(1)} %dynamic-update-slice.10, ...), channel_id=1, replica_groups=mesh['dp'=16,'tensor'=2] {'dp'}, use_global_device_ids=true, to_apply=%add.1 | all-reduce | flops 3072 | bytes 12288 | tf_op jit(solution)/shard_map/while
  1512.1 10.0 all-gather.9.cloned.1.call-done
  1524.0 55.2 %all-gather.7.cloned.1.call-done = bf16[1024,512]{1,0:T(8,128)(2,1)} async-done(((bf16[64,512]{1,0:T(8,128)(2,1)}), bf16[1024,512]{1,0:T(8,128)(2,1)}) %all-gather.7.cloned.1.call-update) | async-done | bytes 1048592 | tf_op jit(solution)/shard_map/while/body/eval_jaxpr/all_gather | solution.py:164
  1581.0 54.9 %all-gather.11.cloned.1.call-done = bf16[1024,512]{1,0:T(8,128)(2,1)} async-done(((bf16[64,512]{1,0:T(8,128)(2,1)}), bf16[1024,512]{1,0:T(8,128)(2,1)}) %all-gather.11.cloned.1.call-update) | async-done | bytes 1048592 | tf_op jit(solution)/shard_map/while/body/eval_jaxpr/all_gather | solution.py:165
  1639.1 53.7 %all-gather.13.cloned.1.call-done = bf16[512,1024]{0,1:T(8,128)(2,1)} async-done(((bf16[512,64]{0,1:T(8,128)(2,1)}), bf16[512,1024]{0,1:T(8,128)(2,1)}) %all-gather.13.cloned.1.call-update) | async-done | bytes 1048592 | tf_op jit(solution)/shard_map/while/body/eval_jaxpr/all_gather | solution.py:172
  1700.5 14.0 all-reduce.20.cloned.1.call-done
  1717.9 76.7 %all-gather.15.cloned.1.call-done = bf16[1024,2048]{1,0:T(8,128)(2,1)} async-done(((bf16[64,2048]{1,0:T(8,128)(2,1)}), bf16[1024,2048]{1,0:T(8,128)(2,1)}) %all-gather.15.cloned.1.call-update) | async-done | bytes 4194320 | tf_op jit(solution)/shard_map/while/body/eval_jaxpr/all_gather | solution.py:166
  1799.4 73.0 %all-gather.17.cloned.1.call-done = bf16[2048,1024]{0,1:T(8,128)(2,1)} async-done(((bf16[2048,64]{0,1:T(8,128)(2,1)}), bf16[2048,1024]{0,1:T(8,128)(2,1)}) %all-gather.17.cloned.1.call-update) | async-done | bytes 4194320 | tf_op jit(solution)/shard_map/while/body/eval_jaxpr/all_gather | solution.py:173
  1872.4 7.0 convolution_convert_fusion.24
  1879.4 5.3 fusion.231
  1887.9 8.6 select_add_fusion.21
  1896.5 8.6 select_add_fusion.26
  1933.3 7.4 all-reduce.24.cloned.1.call-done
  1953.2 9.2 copy.56
  1964.4 65.4 %all-reduce.11 = (f32[1024]{0:T(1024)S(1)}, f32[1024]{0:T(1024)S(1)}, f32[1024]{0:T(1024)S(1)}) all-reduce(f32[1024]{0:T(1024)S(1)} %get-tuple-element.429, f32[1024]{0:T(1024)S(1)} %get-tuple-element.430, f32[1024]{0:T(1024)S(1)} %get-tuple-element.431), channel_id=8, replica_groups=mesh['dp'=16,'tensor'=2] {'dp'}, use_global_device_ids=true, to_apply=%region_24.26.clone | all-reduce | flops 3072 | bytes 24576
  2031.5 72.3 %reduce-scatter.11.cloned.1.call-done = f32[64,512]{1,0:T(8,128)} async-done(((f32[1024,512]{1,0:T(8,128)}), f32[64,512]{1,0:T(8,128)}) %reduce-scatter.11.cloned.1.call-update) | async-done | bytes 131088 | tf_op jit(solution)/shard_map/reduce_scatter | solution.py:205
  2103.9 80.7 %reduce-scatter.7.cloned.1.call-done = f32[64,512]{1,0:T(8,128)} async-done(((f32[1024,512]{1,0:T(8,128)}), f32[64,512]{1,0:T(8,128)}) %reduce-scatter.7.cloned.1.call-update) | async-done | bytes 131088 | tf_op jit(solution)/shard_map/reduce_scatter | solution.py:203
  2184.6 80.9 %reduce-scatter.9.cloned.1.call-done = f32[64,512]{1,0:T(8,128)} async-done(((f32[1024,512]{1,0:T(8,128)}), f32[64,512]{1,0:T(8,128)}) %reduce-scatter.9.cloned.1.call-update) | async-done | bytes 131088 | tf_op jit(solution)/shard_map/reduce_scatter | solution.py:204
  2265.5 190.3 %reduce-scatter.17.cloned.1.call-done = f32[2048,64]{0,1:T(8,128)} async-done(((f32[2048,1024]{0,1:T(8,128)}), f32[2048,64]{0,1:T(8,128)}) %reduce-scatter.17.cloned.1.call-update) | async-done | bytes 524304 | tf_op jit(solution)/shard_map/reduce_scatter | solution.py:213
  2455.9 183.1 %reduce-scatter.15.cloned.1.call-done = f32[64,2048]{1,0:T(8,128)} async-done(((f32[1024,2048]{1,0:T(8,128)}), f32[64,2048]{1,0:T(8,128)}) %reduce-scatter.15.cloned.1.call-update) | async-done | bytes 524304 | tf_op jit(solution)/shard_map/reduce_scatter | solution.py:206
  (719 shorter events, 303.7 us)
Async XLA Ops:
  8.1 59.3 %all-gather.9.cloned.1.call-start = ((), (), s32[]{:S(2)}) async-start(), calls=%async_computation.13 | async-start | bytes 1114112 | tf_op jit(solution)/shard_map/while/body/eval_jaxpr/all_gather | solution.py:163
  8.9 115.6 %all-gather.7.cloned.1.call-start = ((), (), s32[]{:S(2)}) async-start(), calls=%async_computation.12 | async-start | bytes 1114112 | tf_op jit(solution)/shard_map/while/body/eval_jaxpr/all_gather | solution.py:164
  9.6 171.7 %all-gather.11.cloned.1.call-start = ((), (), s32[]{:S(2)}) async-start(), calls=%async_computation.14 | async-start | bytes 1114112 | tf_op jit(solution)/shard_map/while/body/eval_jaxpr/all_gather | solution.py:165
  10.4 227.7 %all-gather.13.cloned.1.call-start = ((), (), s32[]{:S(2)}) async-start(), calls=%async_computation.15 | async-start | bytes 1114112 | tf_op jit(solution)/shard_map/while/body/eval_jaxpr/all_gather | solution.py:172
  10.9 248.7 %all-reduce.20.cloned.1.call-start = ((), (), s32[]{:S(2)}) async-start(), calls=%async_computation.16 | async-start | bytes 1048576 | tf_op jit(solution)/shard_map/while/body/eval_jaxpr/while/body/eval_jaxpr/psum | solution.py:74
  16.8 8.7 copy-start.38
  69.3 113.9 %copy-start.26 = (bf16[256,512]{0,1:T(8,128)(2,1)}, bf16[256,512]{0,1:T(8,128)(2,1)S(1)}, u32[]{:S(2)}) copy-start(bf16[256,512]{0,1:T(8,128)(2,1)S(1)} %copy.66) | copy-start | bytes 786436 | tf_op jit(solution)/shard_map/while
  126.3 57.4 %copy-start.28 = (bf16[256,512]{0,1:T(8,128)(2,1)}, bf16[256,512]{0,1:T(8,128)(2,1)S(1)}, u32[]{:S(2)}) copy-start(bf16[256,512]{0,1:T(8,128)(2,1)S(1)} %copy.65) | copy-start | bytes 786436 | tf_op jit(solution)/shard_map/while
  240.6 99.0 %all-gather.15.cloned.1.call-start = ((), (), s32[]{:S(2)}) async-start(), calls=%async_computation.17 | async-start | bytes 4456448 | tf_op jit(solution)/shard_map/while/body/eval_jaxpr/all_gather | solution.py:166
  241.2 176.3 %all-gather.17.cloned.1.call-start = ((), (), s32[]{:S(2)}) async-start(), calls=%async_computation.18 | async-start | bytes 4456448 | tf_op jit(solution)/shard_map/while/body/eval_jaxpr/all_gather | solution.py:173
  241.9 209.8 %all-reduce.22.cloned.1.call-start = ((), (), s32[]{:S(2)}) async-start(), calls=%async_computation.19 | async-start | bytes 2097152 | tf_op jit(solution)/shard_map/while/body/eval_jaxpr/while/body/eval_jaxpr/psum | solution.py:101
  433.0 52.9 %all-reduce.24.cloned.1.call-start = ((), (), s32[]{:S(2)}) async-start(), calls=%async_computation.20 | async-start | bytes 1048576 | tf_op jit(solution)/shard_map/while/body/eval_jaxpr/while/body/eval_jaxpr/psum | solution.py:146
  477.0 11.2 copy-start.17
  478.5 9.8 copy-start.1
  493.4 58.7 %all-gather.9.cloned.1.call-start = ((), (), s32[]{:S(2)}) async-start(), calls=%async_computation.13 | async-start | bytes 1114112 | tf_op jit(solution)/shard_map/while/body/eval_jaxpr/all_gather | solution.py:163
  494.0 115.2 %all-gather.7.cloned.1.call-start = ((), (), s32[]{:S(2)}) async-start(), calls=%async_computation.12 | async-start | bytes 1114112 | tf_op jit(solution)/shard_map/while/body/eval_jaxpr/all_gather | solution.py:164
  494.7 171.2 %all-gather.11.cloned.1.call-start = ((), (), s32[]{:S(2)}) async-start(), calls=%async_computation.14 | async-start | bytes 1114112 | tf_op jit(solution)/shard_map/while/body/eval_jaxpr/all_gather | solution.py:165
  495.3 227.5 %all-gather.13.cloned.1.call-start = ((), (), s32[]{:S(2)}) async-start(), calls=%async_computation.15 | async-start | bytes 1114112 | tf_op jit(solution)/shard_map/while/body/eval_jaxpr/all_gather | solution.py:172
  496.1 248.3 %all-reduce.20.cloned.1.call-start = ((), (), s32[]{:S(2)}) async-start(), calls=%async_computation.16 | async-start | bytes 1048576 | tf_op jit(solution)/shard_map/while/body/eval_jaxpr/while/body/eval_jaxpr/psum | solution.py:74
  501.9 8.7 copy-start.38
  554.0 113.8 %copy-start.26 = (bf16[256,512]{0,1:T(8,128)(2,1)}, bf16[256,512]{0,1:T(8,128)(2,1)S(1)}, u32[]{:S(2)}) copy-start(bf16[256,512]{0,1:T(8,128)(2,1)S(1)} %copy.66) | copy-start | bytes 786436 | tf_op jit(solution)/shard_map/while
  611.0 57.3 %copy-start.28 = (bf16[256,512]{0,1:T(8,128)(2,1)}, bf16[256,512]{0,1:T(8,128)(2,1)S(1)}, u32[]{:S(2)}) copy-start(bf16[256,512]{0,1:T(8,128)(2,1)S(1)} %copy.65) | copy-start | bytes 786436 | tf_op jit(solution)/shard_map/while
  725.3 99.0 %all-gather.15.cloned.1.call-start = ((), (), s32[]{:S(2)}) async-start(), calls=%async_computation.17 | async-start | bytes 4456448 | tf_op jit(solution)/shard_map/while/body/eval_jaxpr/all_gather | solution.py:166
  725.9 176.2 %all-gather.17.cloned.1.call-start = ((), (), s32[]{:S(2)}) async-start(), calls=%async_computation.18 | async-start | bytes 4456448 | tf_op jit(solution)/shard_map/while/body/eval_jaxpr/all_gather | solution.py:173
  726.5 209.8 %all-reduce.22.cloned.1.call-start = ((), (), s32[]{:S(2)}) async-start(), calls=%async_computation.19 | async-start | bytes 2097152 | tf_op jit(solution)/shard_map/while/body/eval_jaxpr/while/body/eval_jaxpr/psum | solution.py:101
  917.5 52.9 %all-reduce.24.cloned.1.call-start = ((), (), s32[]{:S(2)}) async-start(), calls=%async_computation.20 | async-start | bytes 1048576 | tf_op jit(solution)/shard_map/while/body/eval_jaxpr/while/body/eval_jaxpr/psum | solution.py:146
  917.6 8.6 copy-start.30
  961.5 11.2 copy-start.17
  963.0 9.8 copy-start.1
  978.0 59.0 %all-gather.9.cloned.1.call-start = ((), (), s32[]{:S(2)}) async-start(), calls=%async_computation.13 | async-start | bytes 1114112 | tf_op jit(solution)/shard_map/while/body/eval_jaxpr/all_gather | solution.py:163
  978.7 115.2 %all-gather.7.cloned.1.call-start = ((), (), s32[]{:S(2)}) async-start(), calls=%async_computation.12 | async-start | bytes 1114112 | tf_op jit(solution)/shard_map/while/body/eval_jaxpr/all_gather | solution.py:164
  979.3 171.5 %all-gather.11.cloned.1.call-start = ((), (), s32[]{:S(2)}) async-start(), calls=%async_computation.14 | async-start | bytes 1114112 | tf_op jit(solution)/shard_map/while/body/eval_jaxpr/all_gather | solution.py:165
  980.0 227.6 %all-gather.13.cloned.1.call-start = ((), (), s32[]{:S(2)}) async-start(), calls=%async_computation.15 | async-start | bytes 1114112 | tf_op jit(solution)/shard_map/while/body/eval_jaxpr/all_gather | solution.py:172
  980.8 248.6 %all-reduce.20.cloned.1.call-start = ((), (), s32[]{:S(2)}) async-start(), calls=%async_computation.16 | async-start | bytes 1048576 | tf_op jit(solution)/shard_map/while/body/eval_jaxpr/while/body/eval_jaxpr/psum | solution.py:74
  986.6 8.7 copy-start.38
  1038.8 113.8 %copy-start.26 = (bf16[256,512]{0,1:T(8,128)(2,1)}, bf16[256,512]{0,1:T(8,128)(2,1)S(1)}, u32[]{:S(2)}) copy-start(bf16[256,512]{0,1:T(8,128)(2,1)S(1)} %copy.66) | copy-start | bytes 786436 | tf_op jit(solution)/shard_map/while
  1095.7 57.4 %copy-start.28 = (bf16[256,512]{0,1:T(8,128)(2,1)}, bf16[256,512]{0,1:T(8,128)(2,1)S(1)}, u32[]{:S(2)}) copy-start(bf16[256,512]{0,1:T(8,128)(2,1)S(1)} %copy.65) | copy-start | bytes 786436 | tf_op jit(solution)/shard_map/while
  1210.1 99.2 %all-gather.15.cloned.1.call-start = ((), (), s32[]{:S(2)}) async-start(), calls=%async_computation.17 | async-start | bytes 4456448 | tf_op jit(solution)/shard_map/while/body/eval_jaxpr/all_gather | solution.py:166
  1210.7 176.5 %all-gather.17.cloned.1.call-start = ((), (), s32[]{:S(2)}) async-start(), calls=%async_computation.18 | async-start | bytes 4456448 | tf_op jit(solution)/shard_map/while/body/eval_jaxpr/all_gather | solution.py:173
  1211.5 209.9 %all-reduce.22.cloned.1.call-start = ((), (), s32[]{:S(2)}) async-start(), calls=%async_computation.19 | async-start | bytes 2097152 | tf_op jit(solution)/shard_map/while/body/eval_jaxpr/while/body/eval_jaxpr/psum | solution.py:101
  1402.7 52.9 %all-reduce.24.cloned.1.call-start = ((), (), s32[]{:S(2)}) async-start(), calls=%async_computation.20 | async-start | bytes 1048576 | tf_op jit(solution)/shard_map/while/body/eval_jaxpr/while/body/eval_jaxpr/psum | solution.py:146
  1402.7 8.6 copy-start.30
  1446.7 11.2 copy-start.17
  1448.2 9.8 copy-start.1
  1463.1 59.0 %all-gather.9.cloned.1.call-start = ((), (), s32[]{:S(2)}) async-start(), calls=%async_computation.13 | async-start | bytes 1114112 | tf_op jit(solution)/shard_map/while/body/eval_jaxpr/all_gather | solution.py:163
  1463.9 115.3 %all-gather.7.cloned.1.call-start = ((), (), s32[]{:S(2)}) async-start(), calls=%async_computation.12 | async-start | bytes 1114112 | tf_op jit(solution)/shard_map/while/body/eval_jaxpr/all_gather | solution.py:164
  1464.6 171.3 %all-gather.11.cloned.1.call-start = ((), (), s32[]{:S(2)}) async-start(), calls=%async_computation.14 | async-start | bytes 1114112 | tf_op jit(solution)/shard_map/while/body/eval_jaxpr/all_gather | solution.py:165
  1465.2 227.6 %all-gather.13.cloned.1.call-start = ((), (), s32[]{:S(2)}) async-start(), calls=%async_computation.15 | async-start | bytes 1114112 | tf_op jit(solution)/shard_map/while/body/eval_jaxpr/all_gather | solution.py:172
  1465.9 248.6 %all-reduce.20.cloned.1.call-start = ((), (), s32[]{:S(2)}) async-start(), calls=%async_computation.16 | async-start | bytes 1048576 | tf_op jit(solution)/shard_map/while/body/eval_jaxpr/while/body/eval_jaxpr/psum | solution.py:74
  1471.8 8.7 copy-start.38
  1524.0 113.8 %copy-start.26 = (bf16[256,512]{0,1:T(8,128)(2,1)}, bf16[256,512]{0,1:T(8,128)(2,1)S(1)}, u32[]{:S(2)}) copy-start(bf16[256,512]{0,1:T(8,128)(2,1)S(1)} %copy.66) | copy-start | bytes 786436 | tf_op jit(solution)/shard_map/while
  1581.0 57.3 %copy-start.28 = (bf16[256,512]{0,1:T(8,128)(2,1)}, bf16[256,512]{0,1:T(8,128)(2,1)S(1)}, u32[]{:S(2)}) copy-start(bf16[256,512]{0,1:T(8,128)(2,1)S(1)} %copy.65) | copy-start | bytes 786436 | tf_op jit(solution)/shard_map/while
  1695.3 99.2 %all-gather.15.cloned.1.call-start = ((), (), s32[]{:S(2)}) async-start(), calls=%async_computation.17 | async-start | bytes 4456448 | tf_op jit(solution)/shard_map/while/body/eval_jaxpr/all_gather | solution.py:166
  1695.9 176.5 %all-gather.17.cloned.1.call-start = ((), (), s32[]{:S(2)}) async-start(), calls=%async_computation.18 | async-start | bytes 4456448 | tf_op jit(solution)/shard_map/while/body/eval_jaxpr/all_gather | solution.py:173
  1696.6 209.9 %all-reduce.22.cloned.1.call-start = ((), (), s32[]{:S(2)}) async-start(), calls=%async_computation.19 | async-start | bytes 2097152 | tf_op jit(solution)/shard_map/while/body/eval_jaxpr/while/body/eval_jaxpr/psum | solution.py:101
  1887.8 52.9 %all-reduce.24.cloned.1.call-start = ((), (), s32[]{:S(2)}) async-start(), calls=%async_computation.20 | async-start | bytes 1048576 | tf_op jit(solution)/shard_map/while/body/eval_jaxpr/while/body/eval_jaxpr/psum | solution.py:146
  1931.8 11.2 copy-start.17
  1933.3 9.8 copy-start.1
  1948.3 83.3 %reduce-scatter.13.cloned.1.call-start = ((), (), s32[]{:S(2)}) async-start(), calls=%async_computation.9 | async-start | bytes 2228224 | tf_op jit(solution)/shard_map/reduce_scatter | solution.py:212
  1951.2 152.7 %reduce-scatter.11.cloned.1.call-start = ((), (), s32[]{:S(2)}) async-start(), calls=%async_computation.8 | async-start | bytes 2228224 | tf_op jit(solution)/shard_map/reduce_scatter | solution.py:205
  1951.8 232.8 %reduce-scatter.7.cloned.1.call-start = ((), (), s32[]{:S(2)}) async-start(), calls=%async_computation.6 | async-start | bytes 2228224 | tf_op jit(solution)/shard_map/reduce_scatter | solution.py:203
  1952.4 313.1 %reduce-scatter.9.cloned.1.call-start = ((), (), s32[]{:S(2)}) async-start(), calls=%async_computation.7 | async-start | bytes 2228224 | tf_op jit(solution)/shard_map/reduce_scatter | solution.py:204
  1953.1 502.7 %reduce-scatter.17.cloned.1.call-start = ((), (), s32[]{:S(2)}) async-start(), calls=%async_computation.11 | async-start | bytes 8912896 | tf_op jit(solution)/shard_map/reduce_scatter | solution.py:213
  1962.4 676.5 %reduce-scatter.15.cloned.1.call-start = ((), (), s32[]{:S(2)}) async-start(), calls=%async_computation.10 | async-start | bytes 8912896 | tf_op jit(solution)/shard_map/reduce_scatter | solution.py:206
  (143 other events, 363.5 us)
Sparse Core Ops, SparseCore 0:
  11.7 55.6 all-gather.8
  70.2 54.2 all-gather.6
  127.2 54.0 all-gather.10
  184.0 54.0 all-gather.12
  240.8 18.7 all-reduce.19
  262.6 76.9 all-gather.14
  342.8 74.6 all-gather.16
  433.1 18.5 all-reduce.21
  465.9 19.8 all-reduce.23
  496.7 55.4 all-gather.8
  554.9 54.2 all-gather.6
  611.8 54.0 all-gather.10
  668.7 54.0 all-gather.12
  725.5 18.7 all-reduce.19
  747.3 76.9 all-gather.14
  827.3 74.6 all-gather.16
  917.6 18.5 all-reduce.21
  950.5 19.8 all-reduce.23
  981.6 55.4 all-gather.8
  1039.6 54.2 all-gather.6
  1096.6 54.0 all-gather.10
  1153.5 54.0 all-gather.12
  1210.5 18.7 all-reduce.19
  1232.3 76.9 all-gather.14
  1312.5 74.6 all-gather.16
  1402.8 18.5 all-reduce.21
  1435.6 19.8 all-reduce.23
  1466.7 55.4 all-gather.8
  1524.9 54.2 all-gather.6
  1581.8 54.0 all-gather.10
  1638.7 54.0 all-gather.12
  1695.7 18.7 all-reduce.19
  1717.5 76.9 all-gather.14
  1797.7 74.6 all-gather.16
  1888.0 18.5 all-reduce.21
  1920.8 19.8 all-reduce.23
Sparse Core Ops, SparseCore 1:
  1951.6 72.0 reduce-scatter.12
  2026.4 77.5 reduce-scatter.10
  2106.6 77.9 reduce-scatter.6
  2187.5 78.0 reduce-scatter.8
  2268.4 187.4 reduce-scatter.16
  2458.7 180.1 reduce-scatter.14
where the time goes:
time: 2650 us
  waiting for transfers between devices  2020 us (76%)
  matrix products  212 us (8%)
  blocking collectives  209 us (8%)
  local copies, waits for them, and re-layouts  103 us (4%)
  other arithmetic  83.7 us (3%)
    all_gather x4, waiting for transfers between devices, micro_step(): lax.all_gather(w_up, 'dp', axis=0, tiled=True)  307 us
    all_gather x4, waiting for transfers between devices, micro_step(): lax.all_gather(w_down, 'dp', axis=1, tiled=True)  292 us
    all_gather x4, waiting for transfers between devices, micro_step(): lax.all_gather(w_key, 'dp', axis=0, tiled=True)  221 us
    all_gather x4, waiting for transfers between devices, micro_step(): lax.all_gather(w_value, 'dp', axis=0, tiled=True)  220 us
    all_gather x4, waiting for transfers between devices, micro_step(): lax.all_gather(w_out, 'dp', axis=1, tiled=True)  215 us
    dot_general x76, matrix products, dense(): return jnp.dot(left, right, preferred_element_type=jnp.float32)  200 us
    reduce_scatter x1, waiting for transfers between devices, shards(): lax.psum_scatter(g_down, 'dp', scatter_dimension=1, tiled=True)  190 us
    reduce_scatter x1, waiting for transfers between devices, shards(): lax.psum_scatter(g_up, 'dp', scatter_dimension=0, tiled=True)  183 us
  transfers between devices with their start and end apart: 42, of which 41 were waited for; matrix products, arithmetic and copies ran while one was open for 8% of the time, Pallas kernels for 0%

commit v1 on v0

--- a/solution.py
+++ b/solution.py
@@ -5,6 +5,28 @@
 
 HD = 64
 eps_norm = 1e-05
+
+
+def in_order(pieces, dim):
+    lengths = list(pieces.shape[1:])
+    lengths[dim] *= pieces.shape[0]
+    return jnp.moveaxis(pieces, 0, dim).reshape(lengths)
+
+
+def collected_by_bits(value, axis):
+    size = lax.axis_size(axis)
+    blocks = value[None]
+    for level in range(size.bit_length() - 1):
+        apart = 1 << level
+        partner_block = lax.ppermute(blocks, axis, [(i, i ^ apart) for i in range(size)])
+        both = jnp.stack([blocks, partner_block])
+        upper = lax.axis_index(axis) >> level & 1
+        blocks = jnp.where(upper == 0, both, both[::-1]).reshape(-1, *value.shape)
+    return blocks
+
+
+def doubled_up(value, axis, dim):
+    return in_order(collected_by_bits(value, axis), dim)
 
 
 def rms_norm(values, gain):
@@ -161,7 +183,7 @@
         tok_micro, routed_micro, cot_micro = micro_inputs
         weight_rows = (
             lax.all_gather(w_query, "dp", axis=0, tiled=True),
-            lax.all_gather(w_key, "dp", axis=0, tiled=True),
+            doubled_up(w_key, "dp", 0),
             lax.all_gather(w_value, "dp", axis=0, tiled=True),
             lax.all_gather(w_up, "dp", axis=0, tiled=True),
             lax.all_gather(w_route, "dp", axis=0, tiled=True),

time: 2650 us -> 2500 us (0.943)
  waiting for transfers between devices: 2020 us -> 1780 us
  blocking collectives: 209 us -> 265 us
    all_gather x4 -> x0, waiting for transfers between devices: 221 us -> none  [micro_step(): lax.all_gather(w_key, 'dp', axis=0, tiled=True)]
    reduce_scatter x1, waiting for transfers between devices: 80.7 us -> 0.01 us  [shards(): lax.psum_scatter(g_query, 'dp', scatter_dimension=0, tiled=True)]
    reduce_scatter x1, waiting for transfers between devices: 0.01 us -> 80 us  [shards(): lax.psum_scatter(g_out, 'dp', scatter_dimension=1, tiled=True)]
    while x4, blocking collectives: 126 us -> 181 us
    all_gather x4, waiting for transfers between devices: 39.9 us -> 2.42 us  [micro_step(): lax.all_gather(w_query, 'dp', axis=0, tiled=True)]
  transfers between devices with their start and end apart: 42 -> 51, of which waited for: 41 -> 39; matrix products, arithmetic and copies ran while one was open for 8% -> 9% of each run, Pallas kernels for 0% -> 0%
where the time goes in v1:
time: 2500 us; the launch traced here: 2490 us
  waiting for transfers between devices  1780 us (71%)
  blocking collectives  265 us (11%)
  matrix products  225 us (9%)
  local copies, waits for them, and re-layouts  97.1 us (4%)
  other arithmetic  87.4 us (3%)
    all_gather x4, waiting for transfers between devices, micro_step(): lax.all_gather(w_up, 'dp', axis=0, tiled=True)  307 us
    all_gather x4, waiting for transfers between devices, micro_step(): lax.all_gather(w_down, 'dp', axis=1, tiled=True)  291 us
    all_gather x4, waiting for transfers between devices, micro_step(): lax.all_gather(w_out, 'dp', axis=1, tiled=True)  215 us
    all_gather x4, waiting for transfers between devices, micro_step(): lax.all_gather(w_value, 'dp', axis=0, tiled=True)  214 us
    dot_general x76, matrix products, dense(): return jnp.dot(left, right, preferred_element_type=jnp.float32)  213 us
    reduce_scatter x1, waiting for transfers between devices, shards(): lax.psum_scatter(g_up, 'dp', scatter_dimension=0, tiled=True)  191 us
    reduce_scatter x1, waiting for transfers between devices, shards(): lax.psum_scatter(g_down, 'dp', scatter_dimension=1, tiled=True)  183 us
    while x4, blocking collectives  181 us
  transfers between devices with their start and end apart: 51, of which 39 were waited for; matrix products, arithmetic and copies ran while one was open for 9% of the time, Pallas kernels for 0%

profile of v1, /device:TPU:10, one launch (start us, length us, event | category | flops | bytes accessed | tf_op | source)
XLA Modules:
  0.0 2494.2 jit_solution(11550777376927756982)
XLA Ops:
  8.7 3.9 collective-permute-done.3
  13.4 1783.8 %while.33 = (s32[]{:T(128)}, f32[1024,512]{1,0:T(8,128)}, f32[1024,512]{1,0:T(8,128)}, f32[1024,512]{1,0:T(8,128)}, f32[1024,2048]{1,0:T(8,128)}, /*index=5*/f32...) while((s32[]{:T(128)}, f32[1024,512]{1,0:T(8,128)}, ...), condition=%wide.region_17.19_spmd.clone, body=%wide.region_0.18_spmd.clone.sunk | while | flops 11213889536 | bytes 361085152 | solution.py:221
  17.4 3.8 dynamic-slice_bitcast_fusion.3
  32.8 44.1 %all-reduce.14 = (bf16[1024]{0:T(1024)(128)(2,1)S(1)}, bf16[1024]{0:T(1024)(128)(2,1)S(1)}, bf16[1024]{0:T(1024)(128)(2,1)S(1)}) all-reduce(bf16[1024]{0:T(1024)(128)(2,1)S(1)} %dynamic-update-slice.9, bf16[1024]{0:T(1024)(128)(2,1)S(1)} %dynamic-update-slice.10, ...), channel_id=1, replica_groups=mesh['dp'=16,'tensor'=2] {'dp'}, use_global_device_ids=true, to_apply=%add.1 | all-reduce | flops 3072 | bytes 12288 | tf_op jit(solution)/shard_map/while
  85.5 55.0 %all-gather.8.cloned.1.call-done = bf16[1024,512]{1,0:T(8,128)(2,1)} async-done(((bf16[64,512]{1,0:T(8,128)(2,1)}), bf16[1024,512]{1,0:T(8,128)(2,1)}) %all-gather.8.cloned.1.call-update) | async-done | bytes 1048592 | tf_op jit(solution)/shard_map/while/body/eval_jaxpr/all_gather | solution.py:187
  143.7 53.7 %all-gather.10.cloned.1.call-done = bf16[512,1024]{0,1:T(8,128)(2,1)} async-done(((bf16[512,64]{0,1:T(8,128)(2,1)}), bf16[512,1024]{0,1:T(8,128)(2,1)}) %all-gather.10.cloned.1.call-update) | async-done | bytes 1048592 | tf_op jit(solution)/shard_map/while/body/eval_jaxpr/all_gather | solution.py:194
  205.0 13.9 all-reduce.20.cloned.1.call-done
  222.3 76.7 %all-gather.12.cloned.1.call-done = bf16[1024,2048]{1,0:T(8,128)(2,1)} async-done(((bf16[64,2048]{1,0:T(8,128)(2,1)}), bf16[1024,2048]{1,0:T(8,128)(2,1)}) %all-gather.12.cloned.1.call-update) | async-done | bytes 4194320 | tf_op jit(solution)/shard_map/while/body/eval_jaxpr/all_gather | solution.py:188
  299.0 4.9 fusion.234
  303.9 72.8 %all-gather.14.cloned.1.call-done = bf16[2048,1024]{0,1:T(8,128)(2,1)} async-done(((bf16[2048,64]{0,1:T(8,128)(2,1)}), bf16[2048,1024]{0,1:T(8,128)(2,1)}) %all-gather.14.cloned.1.call-update) | async-done | bytes 4194320 | tf_op jit(solution)/shard_map/while/body/eval_jaxpr/all_gather | solution.py:195
  376.7 7.0 convolution_convert_fusion.24
  383.7 5.3 fusion.235
  392.2 6.1 select_add_fusion.21
  398.3 5.2 select_add_fusion.26
  403.5 7.3 all-reduce.22.cloned.1.call-done
  438.0 13.3 all-reduce.24.cloned.1.call-done
  453.6 3.7 scatter_custom_fusion.13
  462.5 3.8 dynamic-slice_bitcast_fusion.3
  479.9 45.8 %all-reduce.14 = (bf16[1024]{0:T(1024)(128)(2,1)S(1)}, bf16[1024]{0:T(1024)(128)(2,1)S(1)}, bf16[1024]{0:T(1024)(128)(2,1)S(1)}) all-reduce(bf16[1024]{0:T(1024)(128)(2,1)S(1)} %dynamic-update-slice.9, bf16[1024]{0:T(1024)(128)(2,1)S(1)} %dynamic-update-slice.10, ...), channel_id=1, replica_groups=mesh['dp'=16,'tensor'=2] {'dp'}, use_global_device_ids=true, to_apply=%add.1 | all-reduce | flops 3072 | bytes 12288 | tf_op jit(solution)/shard_map/while
  531.9 52.9 %all-gather.8.cloned.1.call-done = bf16[1024,512]{1,0:T(8,128)(2,1)} async-done(((bf16[64,512]{1,0:T(8,128)(2,1)}), bf16[1024,512]{1,0:T(8,128)(2,1)}) %all-gather.8.cloned.1.call-update) | async-done | bytes 1048592 | tf_op jit(solution)/shard_map/while/body/eval_jaxpr/all_gather | solution.py:187
  588.0 53.7 %all-gather.10.cloned.1.call-done = bf16[512,1024]{0,1:T(8,128)(2,1)} async-done(((bf16[512,64]{0,1:T(8,128)(2,1)}), bf16[512,1024]{0,1:T(8,128)(2,1)}) %all-gather.10.cloned.1.call-update) | async-done | bytes 1048592 | tf_op jit(solution)/shard_map/while/body/eval_jaxpr/all_gather | solution.py:194
  649.5 13.8 all-reduce.20.cloned.1.call-done
  666.6 76.8 %all-gather.12.cloned.1.call-done = bf16[1024,2048]{1,0:T(8,128)(2,1)} async-done(((bf16[64,2048]{1,0:T(8,128)(2,1)}), bf16[1024,2048]{1,0:T(8,128)(2,1)}) %all-gather.12.cloned.1.call-update) | async-done | bytes 4194320 | tf_op jit(solution)/shard_map/while/body/eval_jaxpr/all_gather | solution.py:188
  743.4 4.9 fusion.234
  748.3 72.8 %all-gather.14.cloned.1.call-done = bf16[2048,1024]{0,1:T(8,128)(2,1)} async-done(((bf16[2048,64]{0,1:T(8,128)(2,1)}), bf16[2048,1024]{0,1:T(8,128)(2,1)}) %all-gather.14.cloned.1.call-update) | async-done | bytes 4194320 | tf_op jit(solution)/shard_map/while/body/eval_jaxpr/all_gather | solution.py:195
  821.2 7.0 convolution_convert_fusion.24
  828.2 5.3 fusion.235
  836.7 8.6 select_add_fusion.21
  845.2 8.6 select_add_fusion.26
  885.7 11.6 all-reduce.24.cloned.1.call-done
  908.5 3.8 dynamic-slice_bitcast_fusion.3
  925.9 45.8 %all-reduce.14 = (bf16[1024]{0:T(1024)(128)(2,1)S(1)}, bf16[1024]{0:T(1024)(128)(2,1)S(1)}, bf16[1024]{0:T(1024)(128)(2,1)S(1)}) all-reduce(bf16[1024]{0:T(1024)(128)(2,1)S(1)} %dynamic-update-slice.9, bf16[1024]{0:T(1024)(128)(2,1)S(1)} %dynamic-update-slice.10, ...), channel_id=1, replica_groups=mesh['dp'=16,'tensor'=2] {'dp'}, use_global_device_ids=true, to_apply=%add.1 | all-reduce | flops 3072 | bytes 12288 | tf_op jit(solution)/shard_map/while
  978.0 52.9 %all-gather.8.cloned.1.call-done = bf16[1024,512]{1,0:T(8,128)(2,1)} async-done(((bf16[64,512]{1,0:T(8,128)(2,1)}), bf16[1024,512]{1,0:T(8,128)(2,1)}) %all-gather.8.cloned.1.call-update) | async-done | bytes 1048592 | tf_op jit(solution)/shard_map/while/body/eval_jaxpr/all_gather | solution.py:187
  1034.1 53.7 %all-gather.10.cloned.1.call-done = bf16[512,1024]{0,1:T(8,128)(2,1)} async-done(((bf16[512,64]{0,1:T(8,128)(2,1)}), bf16[512,1024]{0,1:T(8,128)(2,1)}) %all-gather.10.cloned.1.call-update) | async-done | bytes 1048592 | tf_op jit(solution)/shard_map/while/body/eval_jaxpr/all_gather | solution.py:194
  1095.7 13.6 all-reduce.20.cloned.1.call-done
  1112.7 76.8 %all-gather.12.cloned.1.call-done = bf16[1024,2048]{1,0:T(8,128)(2,1)} async-done(((bf16[64,2048]{1,0:T(8,128)(2,1)}), bf16[1024,2048]{1,0:T(8,128)(2,1)}) %all-gather.12.cloned.1.call-update) | async-done | bytes 4194320 | tf_op jit(solution)/shard_map/while/body/eval_jaxpr/all_gather | solution.py:188
  1189.5 4.9 fusion.234
  1194.4 73.0 %all-gather.14.cloned.1.call-done = bf16[2048,1024]{0,1:T(8,128)(2,1)} async-done(((bf16[2048,64]{0,1:T(8,128)(2,1)}), bf16[2048,1024]{0,1:T(8,128)(2,1)}) %all-gather.14.cloned.1.call-update) | async-done | bytes 4194320 | tf_op jit(solution)/shard_map/while/body/eval_jaxpr/all_gather | solution.py:195
  1267.4 7.0 convolution_convert_fusion.24
  1274.4 5.3 fusion.235
  1282.9 8.6 select_add_fusion.21
  1291.5 8.6 select_add_fusion.26
  1332.0 11.6 all-reduce.24.cloned.1.call-done
  1354.9 3.8 dynamic-slice_bitcast_fusion.3
  1372.2 45.6 %all-reduce.14 = (bf16[1024]{0:T(1024)(128)(2,1)S(1)}, bf16[1024]{0:T(1024)(128)(2,1)S(1)}, bf16[1024]{0:T(1024)(128)(2,1)S(1)}) all-reduce(bf16[1024]{0:T(1024)(128)(2,1)S(1)} %dynamic-update-slice.9, bf16[1024]{0:T(1024)(128)(2,1)S(1)} %dynamic-update-slice.10, ...), channel_id=1, replica_groups=mesh['dp'=16,'tensor'=2] {'dp'}, use_global_device_ids=true, to_apply=%add.1 | all-reduce | flops 3072 | bytes 12288 | tf_op jit(solution)/shard_map/while
  1424.2 52.9 %all-gather.8.cloned.1.call-done = bf16[1024,512]{1,0:T(8,128)(2,1)} async-done(((bf16[64,512]{1,0:T(8,128)(2,1)}), bf16[1024,512]{1,0:T(8,128)(2,1)}) %all-gather.8.cloned.1.call-update) | async-done | bytes 1048592 | tf_op jit(solution)/shard_map/while/body/eval_jaxpr/all_gather | solution.py:187
  1480.3 53.5 %all-gather.10.cloned.1.call-done = bf16[512,1024]{0,1:T(8,128)(2,1)} async-done(((bf16[512,64]{0,1:T(8,128)(2,1)}), bf16[512,1024]{0,1:T(8,128)(2,1)}) %all-gather.10.cloned.1.call-update) | async-done | bytes 1048592 | tf_op jit(solution)/shard_map/while/body/eval_jaxpr/all_gather | solution.py:194
  1541.6 13.9 all-reduce.20.cloned.1.call-done
  1558.9 76.8 %all-gather.12.cloned.1.call-done = bf16[1024,2048]{1,0:T(8,128)(2,1)} async-done(((bf16[64,2048]{1,0:T(8,128)(2,1)}), bf16[1024,2048]{1,0:T(8,128)(2,1)}) %all-gather.12.cloned.1.call-update) | async-done | bytes 4194320 | tf_op jit(solution)/shard_map/while/body/eval_jaxpr/all_gather | solution.py:188
  1635.7 4.9 fusion.234
  1640.6 72.8 %all-gather.14.cloned.1.call-done = bf16[2048,1024]{0,1:T(8,128)(2,1)} async-done(((bf16[2048,64]{0,1:T(8,128)(2,1)}), bf16[2048,1024]{0,1:T(8,128)(2,1)}) %all-gather.14.cloned.1.call-update) | async-done | bytes 4194320 | tf_op jit(solution)/shard_map/while/body/eval_jaxpr/all_gather | solution.py:195
  1713.4 7.0 convolution_convert_fusion.24
  1720.4 5.3 fusion.235
  1728.9 8.6 select_add_fusion.21
  1737.5 8.6 select_add_fusion.26
  1778.0 11.6 all-reduce.24.cloned.1.call-done
  1792.0 3.7 scatter_custom_fusion.13
  1802.1 9.3 copy.56
  1813.2 65.5 %all-reduce.11 = (f32[1024]{0:T(1024)S(1)}, f32[1024]{0:T(1024)S(1)}, f32[1024]{0:T(1024)S(1)}) all-reduce(f32[1024]{0:T(1024)S(1)} %get-tuple-element.432, f32[1024]{0:T(1024)S(1)} %get-tuple-element.433, f32[1024]{0:T(1024)S(1)} %get-tuple-element.434), channel_id=8, replica_groups=mesh['dp'=16,'tensor'=2] {'dp'}, use_global_device_ids=true, to_apply=%region_24.26.clone | all-reduce | flops 3072 | bytes 24576
  1880.5 72.0 %reduce-scatter.9.cloned.1.call-done = f32[64,512]{1,0:T(8,128)} async-done(((f32[1024,512]{1,0:T(8,128)}), f32[64,512]{1,0:T(8,128)}) %reduce-scatter.9.cloned.1.call-update) | async-done | bytes 131088 | tf_op jit(solution)/shard_map/reduce_scatter | solution.py:226
  1952.5 80.9 %reduce-scatter.11.cloned.1.call-done = f32[64,512]{1,0:T(8,128)} async-done(((f32[1024,512]{1,0:T(8,128)}), f32[64,512]{1,0:T(8,128)}) %reduce-scatter.11.cloned.1.call-update) | async-done | bytes 131088 | tf_op jit(solution)/shard_map/reduce_scatter | solution.py:227
  2033.3 80.0 %reduce-scatter.13.cloned.1.call-done = f32[512,64]{0,1:T(8,128)} async-done(((f32[512,1024]{0,1:T(8,128)}), f32[512,64]{0,1:T(8,128)}) %reduce-scatter.13.cloned.1.call-update) | async-done | bytes 131088 | tf_op jit(solution)/shard_map/reduce_scatter | solution.py:234
  2113.4 190.6 %reduce-scatter.15.cloned.1.call-done = f32[64,2048]{1,0:T(8,128)} async-done(((f32[1024,2048]{1,0:T(8,128)}), f32[64,2048]{1,0:T(8,128)}) %reduce-scatter.15.cloned.1.call-update) | async-done | bytes 524304 | tf_op jit(solution)/shard_map/reduce_scatter | solution.py:228
  2304.0 183.1 %reduce-scatter.17.cloned.1.call-done = f32[2048,64]{0,1:T(8,128)} async-done(((f32[2048,1024]{0,1:T(8,128)}), f32[2048,64]{0,1:T(8,128)}) %reduce-scatter.17.cloned.1.call-update) | async-done | bytes 524304 | tf_op jit(solution)/shard_map/reduce_scatter | solution.py:235
  (700 shorter events, 314.1 us)
Async XLA Ops:
  8.0 4.5 collective-permute-start.3
  13.4 70.2 %all-gather.6.cloned.1.call-start = ((), (), s32[]{:S(2)}) async-start(), calls=%async_computation.12 | async-start | bytes 1114112 | tf_op jit(solution)/shard_map/while/body/eval_jaxpr/all_gather | solution.py:185
  14.2 126.3 %all-gather.8.cloned.1.call-start = ((), (), s32[]{:S(2)}) async-start(), calls=%async_computation.13 | async-start | bytes 1114112 | tf_op jit(solution)/shard_map/while/body/eval_jaxpr/all_gather | solution.py:187
  14.9 182.5 %all-gather.10.cloned.1.call-start = ((), (), s32[]{:S(2)}) async-start(), calls=%async_computation.14 | async-start | bytes 1114112 | tf_op jit(solution)/shard_map/while/body/eval_jaxpr/all_gather | solution.py:194
  15.0 6.2 collective-permute-start
  16.6 202.3 %all-reduce.20.cloned.1.call-start = ((), (), s32[]{:S(2)}) async-start(), calls=%async_computation.15 | async-start | bytes 1048576 | tf_op jit(solution)/shard_map/while/body/eval_jaxpr/while/body/eval_jaxpr/psum | solution.py:96
  21.3 6.7 collective-permute-start.1
  27.0 52.5 %copy-start.17 = (bf16[256,512]{1,0:T(8,128)(2,1)}, bf16[256,512]{1,0:T(8,128)(2,1)S(1)}, u32[]{:S(2)}) copy-start(bf16[256,512]{1,0:T(8,128)(2,1)S(1)} %get-tuple-element.776) | copy-start | bytes 786436 | tf_op jit(solution)/shard_map/while
  28.2 51.2 %collective-permute-start.2 = (bf16[8,64,512]{2,1,0:T(8,128)(2,1)S(1)}, bf16[8,64,512]{2,1,0:T(8,128)(2,1)S(1)}, u32[]{:S(2)}, u32[]{:S(2)}) collective-permute-start(bf16[8,64,512]{2,1,0:T(8,128)(2,1)S(1)} %bitcast.248), channel_id=1, source_target_pairs={{0,16},{2,18},{4,20},{6,22},{8,24},{10,26},{12,28},{14,30},{16,0},... | collective-permute-start | bytes 1572872 | tf_op jit(solution)/shard_map/while/body/eval_jaxpr/ppermute | solution.py:21
  81.3 61.1 %copy-start.18 = (bf16[256,512]{0,1:T(8,128)(2,1)}, bf16[256,512]{0,1:T(8,128)(2,1)S(1)}, u32[]{:S(2)}) copy-start(bf16[256,512]{0,1:T(8,128)(2,1)S(1)} %copy.65) | copy-start | bytes 786436 | tf_op jit(solution)/shard_map/while
  85.5 57.4 %copy-start.20 = (bf16[256,512]{0,1:T(8,128)(2,1)}, bf16[256,512]{0,1:T(8,128)(2,1)S(1)}, u32[]{:S(2)}) copy-start(bf16[256,512]{0,1:T(8,128)(2,1)S(1)} %copy.66) | copy-start | bytes 786436 | tf_op jit(solution)/shard_map/while
  199.9 99.0 %all-gather.12.cloned.1.call-start = ((), (), s32[]{:S(2)}) async-start(), calls=%async_computation.16 | async-start | bytes 4456448 | tf_op jit(solution)/shard_map/while/body/eval_jaxpr/all_gather | solution.py:188
  200.5 176.2 %all-gather.14.cloned.1.call-start = ((), (), s32[]{:S(2)}) async-start(), calls=%async_computation.17 | async-start | bytes 4456448 | tf_op jit(solution)/shard_map/while/body/eval_jaxpr/all_gather | solution.py:195
  201.1 209.7 %all-reduce.22.cloned.1.call-start = ((), (), s32[]{:S(2)}) async-start(), calls=%async_computation.18 | async-start | bytes 2097152 | tf_op jit(solution)/shard_map/while/body/eval_jaxpr/while/body/eval_jaxpr/psum | solution.py:123
  392.1 59.1 %all-reduce.24.cloned.1.call-start = ((), (), s32[]{:S(2)}) async-start(), calls=%async_computation.19 | async-start | bytes 1048576 | tf_op jit(solution)/shard_map/while/body/eval_jaxpr/while/body/eval_jaxpr/psum | solution.py:168
  436.5 17.1 copy-start.16
  458.8 71.2 %all-gather.6.cloned.1.call-start = ((), (), s32[]{:S(2)}) async-start(), calls=%async_computation.12 | async-start | bytes 1114112 | tf_op jit(solution)/shard_map/while/body/eval_jaxpr/all_gather | solution.py:185
  459.5 125.3 %all-gather.8.cloned.1.call-start = ((), (), s32[]{:S(2)}) async-start(), calls=%async_computation.13 | async-start | bytes 1114112 | tf_op jit(solution)/shard_map/while/body/eval_jaxpr/all_gather | solution.py:187
  460.1 181.6 %all-gather.10.cloned.1.call-start = ((), (), s32[]{:S(2)}) async-start(), calls=%async_computation.14 | async-start | bytes 1114112 | tf_op jit(solution)/shard_map/while/body/eval_jaxpr/all_gather | solution.py:194
  460.2 6.2 collective-permute-start
  461.8 201.5 %all-reduce.20.cloned.1.call-start = ((), (), s32[]{:S(2)}) async-start(), calls=%async_computation.15 | async-start | bytes 1048576 | tf_op jit(solution)/shard_map/while/body/eval_jaxpr/while/body/eval_jaxpr/psum | solution.py:96
  466.5 8.7 collective-permute-start.1
  472.2 55.9 %copy-start.17 = (bf16[256,512]{1,0:T(8,128)(2,1)}, bf16[256,512]{1,0:T(8,128)(2,1)S(1)}, u32[]{:S(2)}) copy-start(bf16[256,512]{1,0:T(8,128)(2,1)S(1)} %get-tuple-element.776) | copy-start | bytes 786436 | tf_op jit(solution)/shard_map/while
  475.4 52.6 %collective-permute-start.2 = (bf16[8,64,512]{2,1,0:T(8,128)(2,1)S(1)}, bf16[8,64,512]{2,1,0:T(8,128)(2,1)S(1)}, u32[]{:S(2)}, u32[]{:S(2)}) collective-permute-start(bf16[8,64,512]{2,1,0:T(8,128)(2,1)S(1)} %bitcast.248), channel_id=1, source_target_pairs={{0,16},{2,18},{4,20},{6,22},{8,24},{10,26},{12,28},{14,30},{16,0},... | collective-permute-start | bytes 1572872 | tf_op jit(solution)/shard_map/while/body/eval_jaxpr/ppermute | solution.py:21
  530.0 56.7 %copy-start.18 = (bf16[256,512]{0,1:T(8,128)(2,1)}, bf16[256,512]{0,1:T(8,128)(2,1)S(1)}, u32[]{:S(2)}) copy-start(bf16[256,512]{0,1:T(8,128)(2,1)S(1)} %copy.65) | copy-start | bytes 786436 | tf_op jit(solution)/shard_map/while
  531.9 55.3 %copy-start.20 = (bf16[256,512]{0,1:T(8,128)(2,1)}, bf16[256,512]{0,1:T(8,128)(2,1)S(1)}, u32[]{:S(2)}) copy-start(bf16[256,512]{0,1:T(8,128)(2,1)S(1)} %copy.66) | copy-start | bytes 786436 | tf_op jit(solution)/shard_map/while
  644.2 99.2 %all-gather.12.cloned.1.call-start = ((), (), s32[]{:S(2)}) async-start(), calls=%async_computation.16 | async-start | bytes 4456448 | tf_op jit(solution)/shard_map/while/body/eval_jaxpr/all_gather | solution.py:188
  645.0 176.2 %all-gather.14.cloned.1.call-start = ((), (), s32[]{:S(2)}) async-start(), calls=%async_computation.17 | async-start | bytes 4456448 | tf_op jit(solution)/shard_map/while/body/eval_jaxpr/all_gather | solution.py:195
  645.6 209.7 %all-reduce.22.cloned.1.call-start = ((), (), s32[]{:S(2)}) async-start(), calls=%async_computation.18 | async-start | bytes 2097152 | tf_op jit(solution)/shard_map/while/body/eval_jaxpr/while/body/eval_jaxpr/psum | solution.py:123
  836.6 60.8 %all-reduce.24.cloned.1.call-start = ((), (), s32[]{:S(2)}) async-start(), calls=%async_computation.19 | async-start | bytes 1048576 | tf_op jit(solution)/shard_map/while/body/eval_jaxpr/while/body/eval_jaxpr/psum | solution.py:168
  904.9 71.1 %all-gather.6.cloned.1.call-start = ((), (), s32[]{:S(2)}) async-start(), calls=%async_computation.12 | async-start | bytes 1114112 | tf_op jit(solution)/shard_map/while/body/eval_jaxpr/all_gather | solution.py:185
  905.5 125.4 %all-gather.8.cloned.1.call-start = ((), (), s32[]{:S(2)}) async-start(), calls=%async_computation.13 | async-start | bytes 1114112 | tf_op jit(solution)/shard_map/while/body/eval_jaxpr/all_gather | solution.py:187
  906.1 181.7 %all-gather.10.cloned.1.call-start = ((), (), s32[]{:S(2)}) async-start(), calls=%async_computation.14 | async-start | bytes 1114112 | tf_op jit(solution)/shard_map/while/body/eval_jaxpr/all_gather | solution.py:194
  906.2 6.2 collective-permute-start
  907.7 201.6 %all-reduce.20.cloned.1.call-start = ((), (), s32[]{:S(2)}) async-start(), calls=%async_computation.15 | async-start | bytes 1048576 | tf_op jit(solution)/shard_map/while/body/eval_jaxpr/while/body/eval_jaxpr/psum | solution.py:96
  912.5 8.7 collective-permute-start.1
  918.2 56.0 %copy-start.17 = (bf16[256,512]{1,0:T(8,128)(2,1)}, bf16[256,512]{1,0:T(8,128)(2,1)S(1)}, u32[]{:S(2)}) copy-start(bf16[256,512]{1,0:T(8,128)(2,1)S(1)} %get-tuple-element.776) | copy-start | bytes 786436 | tf_op jit(solution)/shard_map/while
  921.4 52.7 %collective-permute-start.2 = (bf16[8,64,512]{2,1,0:T(8,128)(2,1)S(1)}, bf16[8,64,512]{2,1,0:T(8,128)(2,1)S(1)}, u32[]{:S(2)}, u32[]{:S(2)}) collective-permute-start(bf16[8,64,512]{2,1,0:T(8,128)(2,1)S(1)} %bitcast.248), channel_id=1, source_target_pairs={{0,16},{2,18},{4,20},{6,22},{8,24},{10,26},{12,28},{14,30},{16,0},... | collective-permute-start | bytes 1572872 | tf_op jit(solution)/shard_map/while/body/eval_jaxpr/ppermute | solution.py:21
  976.0 56.7 %copy-start.18 = (bf16[256,512]{0,1:T(8,128)(2,1)}, bf16[256,512]{0,1:T(8,128)(2,1)S(1)}, u32[]{:S(2)}) copy-start(bf16[256,512]{0,1:T(8,128)(2,1)S(1)} %copy.65) | copy-start | bytes 786436 | tf_op jit(solution)/shard_map/while
  978.0 55.3 %copy-start.20 = (bf16[256,512]{0,1:T(8,128)(2,1)}, bf16[256,512]{0,1:T(8,128)(2,1)S(1)}, u32[]{:S(2)}) copy-start(bf16[256,512]{0,1:T(8,128)(2,1)S(1)} %copy.66) | copy-start | bytes 786436 | tf_op jit(solution)/shard_map/while
  1090.3 99.2 %all-gather.12.cloned.1.call-start = ((), (), s32[]{:S(2)}) async-start(), calls=%async_computation.16 | async-start | bytes 4456448 | tf_op jit(solution)/shard_map/while/body/eval_jaxpr/all_gather | solution.py:188
  1091.1 176.3 %all-gather.14.cloned.1.call-start = ((), (), s32[]{:S(2)}) async-start(), calls=%async_computation.17 | async-start | bytes 4456448 | tf_op jit(solution)/shard_map/while/body/eval_jaxpr/all_gather | solution.py:195
  1091.8 209.7 %all-reduce.22.cloned.1.call-start = ((), (), s32[]{:S(2)}) async-start(), calls=%async_computation.18 | async-start | bytes 2097152 | tf_op jit(solution)/shard_map/while/body/eval_jaxpr/while/body/eval_jaxpr/psum | solution.py:123
  1282.8 60.8 %all-reduce.24.cloned.1.call-start = ((), (), s32[]{:S(2)}) async-start(), calls=%async_computation.19 | async-start | bytes 1048576 | tf_op jit(solution)/shard_map/while/body/eval_jaxpr/while/body/eval_jaxpr/psum | solution.py:168
  1351.2 71.1 %all-gather.6.cloned.1.call-start = ((), (), s32[]{:S(2)}) async-start(), calls=%async_computation.12 | async-start | bytes 1114112 | tf_op jit(solution)/shard_map/while/body/eval_jaxpr/all_gather | solution.py:185
  1351.9 125.2 %all-gather.8.cloned.1.call-start = ((), (), s32[]{:S(2)}) async-start(), calls=%async_computation.13 | async-start | bytes 1114112 | tf_op jit(solution)/shard_map/while/body/eval_jaxpr/all_gather | solution.py:187
  1352.5 181.3 %all-gather.10.cloned.1.call-start = ((), (), s32[]{:S(2)}) async-start(), calls=%async_computation.14 | async-start | bytes 1114112 | tf_op jit(solution)/shard_map/while/body/eval_jaxpr/all_gather | solution.py:194
  1352.6 6.2 collective-permute-start
  1354.1 201.4 %all-reduce.20.cloned.1.call-start = ((), (), s32[]{:S(2)}) async-start(), calls=%async_computation.15 | async-start | bytes 1048576 | tf_op jit(solution)/shard_map/while/body/eval_jaxpr/while/body/eval_jaxpr/psum | solution.py:96
  1358.8 8.7 collective-permute-start.1
  1364.6 55.8 %copy-start.17 = (bf16[256,512]{1,0:T(8,128)(2,1)}, bf16[256,512]{1,0:T(8,128)(2,1)S(1)}, u32[]{:S(2)}) copy-start(bf16[256,512]{1,0:T(8,128)(2,1)S(1)} %get-tuple-element.776) | copy-start | bytes 786436 | tf_op jit(solution)/shard_map/while
  1367.7 52.5 %collective-permute-start.2 = (bf16[8,64,512]{2,1,0:T(8,128)(2,1)S(1)}, bf16[8,64,512]{2,1,0:T(8,128)(2,1)S(1)}, u32[]{:S(2)}, u32[]{:S(2)}) collective-permute-start(bf16[8,64,512]{2,1,0:T(8,128)(2,1)S(1)} %bitcast.248), channel_id=1, source_target_pairs={{0,16},{2,18},{4,20},{6,22},{8,24},{10,26},{12,28},{14,30},{16,0},... | collective-permute-start | bytes 1572872 | tf_op jit(solution)/shard_map/while/body/eval_jaxpr/ppermute | solution.py:21
  1422.2 56.7 %copy-start.18 = (bf16[256,512]{0,1:T(8,128)(2,1)}, bf16[256,512]{0,1:T(8,128)(2,1)S(1)}, u32[]{:S(2)}) copy-start(bf16[256,512]{0,1:T(8,128)(2,1)S(1)} %copy.65) | copy-start | bytes 786436 | tf_op jit(solution)/shard_map/while
  1424.2 55.3 %copy-start.20 = (bf16[256,512]{0,1:T(8,128)(2,1)}, bf16[256,512]{0,1:T(8,128)(2,1)S(1)}, u32[]{:S(2)}) copy-start(bf16[256,512]{0,1:T(8,128)(2,1)S(1)} %copy.66) | copy-start | bytes 786436 | tf_op jit(solution)/shard_map/while
  1536.3 99.3 %all-gather.12.cloned.1.call-start = ((), (), s32[]{:S(2)}) async-start(), calls=%async_computation.16 | async-start | bytes 4456448 | tf_op jit(solution)/shard_map/while/body/eval_jaxpr/all_gather | solution.py:188
  1537.1 176.3 %all-gather.14.cloned.1.call-start = ((), (), s32[]{:S(2)}) async-start(), calls=%async_computation.17 | async-start | bytes 4456448 | tf_op jit(solution)/shard_map/while/body/eval_jaxpr/all_gather | solution.py:195
  1537.7 209.9 %all-reduce.22.cloned.1.call-start = ((), (), s32[]{:S(2)}) async-start(), calls=%async_computation.18 | async-start | bytes 2097152 | tf_op jit(solution)/shard_map/while/body/eval_jaxpr/while/body/eval_jaxpr/psum | solution.py:123
  1728.8 60.8 %all-reduce.24.cloned.1.call-start = ((), (), s32[]{:S(2)}) async-start(), calls=%async_computation.19 | async-start | bytes 1048576 | tf_op jit(solution)/shard_map/while/body/eval_jaxpr/while/body/eval_jaxpr/psum | solution.py:168
  1797.2 83.3 %reduce-scatter.7.cloned.1.call-start = ((), (), s32[]{:S(2)}) async-start(), calls=%async_computation.6 | async-start | bytes 2228224 | tf_op jit(solution)/shard_map/reduce_scatter | solution.py:225
  1797.7 154.7 %reduce-scatter.9.cloned.1.call-start = ((), (), s32[]{:S(2)}) async-start(), calls=%async_computation.7 | async-start | bytes 2228224 | tf_op jit(solution)/shard_map/reduce_scatter | solution.py:226
  1798.3 235.0 %reduce-scatter.11.cloned.1.call-start = ((), (), s32[]{:S(2)}) async-start(), calls=%async_computation.8 | async-start | bytes 2228224 | tf_op jit(solution)/shard_map/reduce_scatter | solution.py:227
  1798.9 314.5 %reduce-scatter.13.cloned.1.call-start = ((), (), s32[]{:S(2)}) async-start(), calls=%async_computation.9 | async-start | bytes 2228224 | tf_op jit(solution)/shard_map/reduce_scatter | solution.py:234
  1801.3 502.7 %reduce-scatter.15.cloned.1.call-start = ((), (), s32[]{:S(2)}) async-start(), calls=%async_computation.10 | async-start | bytes 8912896 | tf_op jit(solution)/shard_map/reduce_scatter | solution.py:228
  1802.0 685.0 %reduce-scatter.17.cloned.1.call-start = ((), (), s32[]{:S(2)}) async-start(), calls=%async_computation.11 | async-start | bytes 8912896 | tf_op jit(solution)/shard_map/reduce_scatter | solution.py:235
  (121 other events, 463.9 us)
Sparse Core Ops, SparseCore 0:
  17.0 66.6 all-gather.5
  86.4 54.0 all-gather.7
  143.3 54.0 all-gather.9
  200.2 18.7 all-reduce.19
  222.0 76.9 all-gather.11
  302.0 74.6 all-gather.13
  392.2 18.5 all-reduce.21
  431.3 19.8 all-reduce.23
  462.4 65.7 all-gather.5
  530.8 53.9 all-gather.7
  587.6 54.0 all-gather.9
  644.5 18.7 all-reduce.19
  666.4 76.9 all-gather.11
  746.4 74.6 all-gather.13
  836.7 18.5 all-reduce.21
  877.4 19.8 all-reduce.23
  908.2 66.0 all-gather.5
  976.9 53.9 all-gather.7
  1033.7 54.0 all-gather.9
  1090.5 18.7 all-reduce.19
  1112.5 76.9 all-gather.11
  1192.6 74.6 all-gather.13
  1282.9 18.5 all-reduce.21
  1323.6 19.8 all-reduce.23
  1354.8 65.6 all-gather.5
  1423.1 53.9 all-gather.7
  1479.7 54.0 all-gather.9
  1536.7 18.7 all-reduce.19
  1558.7 76.9 all-gather.11
  1638.7 74.6 all-gather.13
  1728.9 18.5 all-reduce.21
  1769.7 19.8 all-reduce.23
Sparse Core Ops, SparseCore 1:
  1800.5 72.3 reduce-scatter.6
  1875.5 76.9 reduce-scatter.8
  1955.2 78.1 reduce-scatter.10
  2036.2 77.1 reduce-scatter.12
  2116.3 187.7 reduce-scatter.14
  2306.9 180.1 reduce-scatter.16
